TPU v7x, 32 devices: a whole 2x2x4 slice. The times are simulated.
32 devices in a mesh: str: 8 (over z, x), fac: 4 (over y, core).
Axes of the slice: x: 2, y: 2, z: 4, core: 2. Of those that a mesh axis runs over, the one named last changes fastest.
Arguments:
- amplitudes: bfloat16 [2, 4096, 4096], P(None, 'str'), may hold values from -6 to 6
- beta_index: int32 [2, 32, 12], replicated, may hold values from 0 to 31, all different within a row; in each aligned block of 32 rows (0 to 31, 32 to 63, ..., all dimensions but the last counted through in order) at most 24 rows name the same one
- beta_tile: int32 [2, 12], replicated, may hold values from 0 to 15
- beta_flip: int32 [2, 4096], replicated, may hold values 0 or 1
- alpha_index: int32 [2, 32, 12], replicated, may hold values from 0 to 31, all different within a row; in each aligned block of 32 rows (0 to 31, 32 to 63, ..., all dimensions but the last counted through in order) at most 24 rows name the same one
- alpha_tile: int32 [2, 12], replicated, may hold values from 0 to 15
- alpha_flip: int32 [2, 4096], replicated, may hold values 0 or 1
- beta_tiles: bfloat16 [16, 128, 128], replicated, may hold values from -0.15625 to 0.15625
- alpha_tiles: bfloat16 [16, 128, 128], replicated, may hold values from -0.109375 to 0.109375
Outputs:
- sigma: float32 [2, 4096, 4096], P(None, 'fac', 'str')
Inputs may be any that keep to these rules, and one draw needn't show every extreme that they name: `beta_index`: each block row of one factor's beta operator names 12 different block columns; within one factor's operator no block column is named by more than 24 block rows, and in some factor one column is named by exactly 24. `alpha_index`: each block row of one factor's alpha operator names 12 different block columns; within one factor's operator no block column is named by more than 24 block rows, and in some factor one column is named by exactly 24.
All inputs are finite; a program needn't handle non-finite values.
Results may differ from a plain program's by a relative error of at most 0.012.
Values may be sent and summed in bfloat16 or wider, within the bound.
A program may use at most 128 MiB of HBM per device.

v0:
```python
import jax
import jax.numpy as jnp
from jax import lax
from jax.sharding import PartitionSpec as P


def apply_beta(amplitudes, block_ids, tile_ids, flips, tile_table):
    part_count, height, column_count = amplitudes.shape
    tile_size = tile_table.shape[1]
    block_count = column_count // tile_size
    signs = (1 - 2 * flips).astype(jnp.bfloat16)
    signed = amplitudes * signs[None, None, :]
    blocks = signed.reshape(part_count, height, block_count, tile_size)
    weights = tile_table[tile_ids]
    group_size = block_count // 4
    pieces = []
    for group_id in range(4):
        lower = group_id * group_size
        chosen = block_ids[lower : lower + group_size]
        gathered = blocks[:, :, chosen]
        pieces.append(
            jnp.einsum(
                "pajkc,krc->pajr", gathered, weights, preferred_element_type=jnp.float32
            ).astype(jnp.bfloat16)
        )
    return jnp.concatenate(pieces, axis=2).reshape(part_count, height, column_count)


def apply_alpha(half, block_ids, tile_ids, flips, tile_table):
    part_count, total, column_count = half.shape
    tile_size = tile_table.shape[1]
    block_count = total // tile_size
    signs = (1 - 2 * flips).astype(jnp.bfloat16)
    signed = half * signs[None, :, None]
    blocks = signed.reshape(part_count, block_count, tile_size, column_count)
    weights = tile_table[tile_ids]
    group_size = block_count // 4
    pieces = []
    for group_id in range(4):
        lower = group_id * group_size
        chosen = block_ids[lower : lower + group_size]
        gathered = blocks[:, chosen]
        pieces.append(
            jnp.einsum(
                "pjkcn,krc->pjrn", gathered, weights, preferred_element_type=jnp.float32
            ).astype(jnp.bfloat16)
        )
    return jnp.concatenate(pieces, axis=1).reshape(part_count, total, column_count)


def local(
    amplitudes,
    beta_index,
    beta_tile,
    beta_flip,
    alpha_index,
    alpha_tile,
    alpha_flip,
    beta_tiles,
    alpha_tiles,
):
    position = lax.axis_index("fac")
    factor = position // 2
    part = position % 2
    own_part = lax.dynamic_index_in_dim(amplitudes, part, 0, keepdims=True)
    beta_ids = lax.dynamic_index_in_dim(beta_index, factor, 0, keepdims=False)
    beta_kinds = lax.dynamic_index_in_dim(beta_tile, factor, 0, keepdims=False)
    beta_signs = lax.dynamic_index_in_dim(beta_flip, factor, 0, keepdims=False)
    half = apply_beta(own_part, beta_ids, beta_kinds, beta_signs, beta_tiles)
    alpha_ids = lax.dynamic_index_in_dim(alpha_index, factor, 0, keepdims=False)
    alpha_kinds = lax.dynamic_index_in_dim(alpha_tile, factor, 0, keepdims=False)
    alpha_signs = lax.dynamic_index_in_dim(alpha_flip, factor, 0, keepdims=False)
    mixed = apply_alpha(
        lax.all_to_all(half, "str", split_axis=2, concat_axis=1, tiled=True),
        alpha_ids,
        alpha_kinds,
        alpha_signs,
        alpha_tiles,
    )
    mixed = lax.optimization_barrier(mixed)
    selector = (jnp.arange(2) == part)[:, None, None]
    padded = jnp.where(selector, mixed.astype(jnp.float32), 0.0)
    return lax.psum_scatter(
        padded.astype(jnp.bfloat16), "fac", scatter_dimension=1, tiled=True
    ).astype(jnp.float32)


def solution(mesh):
    return jax.shard_map(
        local,
        mesh=mesh,
        in_specs=(P(None, "str", None), P(), P(), P(), P(), P(), P(), P(), P()),
        out_specs=P(None, "fac", "str"),
        check_vma=False,
    )
```

profile of v0, /device:TPU:0, one launch (start us, length us, event | category | flops | bytes accessed | tf_op | source)
XLA Modules:
  0.0 445.0 jit_solution(6631989853623679221)
XLA Ops:
  6.5 4.8 %constant_dynamic-slice_fusion.9 = bf16[1,512,4096]{2,1,0:T(8,128)(2,1)} fusion(bf16[2,512,4096]{2,1,0:T(8,128)(2,1)} %param.9, s32[]{:T(128)S(6)} %select_n.134), kind=kLoop, calls=%fused_computation.69 | loop fusion | bytes 8388612 | tf_op jit(solution)/shard_map/jit(dynamic_index_in_dim)/dynamic_slice | solution.py:65
  11.3 6.5 %copy.44 = bf16[1,512,4096]{1,2,0:T(8,128)(2,1)} copy(bf16[1,512,4096]{2,1,0:T(8,128)(2,1)} %constant_dynamic-slice_fusion.9) | data formatting | bytes 8388608
  17.8 0.1 convert_reduce_fusion
  17.9 4.0 broadcast_multiply_fusion
  21.9 6.4 %copy.28 = bf16[512,32,128]{2,0,1:T(8,128)(2,1)} copy(bf16[512,32,128]{0,2,1:T(8,128)(2,1)} %bitcast.181) | data formatting | bytes 8388608 | tf_op jit(solution)/shard_map/reshape | solution.py:13
  28.3 0.1 constant_dynamic-slice_fusion.5
  28.4 0.1 copy.46
  28.6 0.1 reshape.415
  28.8 9.0 %gather_fusion.1 = bf16[96,512,128]{2,1,0:T(8,128)(2,1)} fusion(bf16[512,32,128]{2,0,1:T(8,128)(2,1)} %copy.28, s32[1024]{0:T(1024)S(1)} %pad_clamp_fusion.8), kind=kCustom, calls=%fused_computation.1 | custom fusion | bytes 25166208 | tf_op jit(solution)/shard_map/gather | solution.py:20
  37.8 9.0 %gather_fusion.3 = bf16[96,512,128]{2,1,0:T(8,128)(2,1)} fusion(bf16[512,32,128]{2,0,1:T(8,128)(2,1)} %copy.28, s32[1024]{0:T(1024)S(1)} %pad_clamp_fusion.6), kind=kCustom, calls=%fused_computation.3 | custom fusion | bytes 25166208 | tf_op jit(solution)/shard_map/gather | solution.py:20
  46.8 0.6 gather_fusion.2
  47.5 8.9 %fusion = bf16[1,512,8,128]{1,3,2,0:T(8,128)(2,1)S(1)} fusion(bf16[512,8,12,128]{3,0,2,1:T(8,128)(2,1)} %bitcast.174, bf16[12,128,128]{2,1,0:T(8,128)(2,1)S(1)} %gather_fusion.2), kind=kOutput, calls=%fused_computation.24 | convolution fusion | flops 1611137024 | bytes 14024704 | tf_op jit(solution)/shard_map/pajkc,krc->pajr/dot_general | solution.py:22
  56.3 4.2 fusion.1
  60.5 0.1 copy.48
  60.7 0.1 reshape.443
  60.8 9.0 %gather_fusion.4 = bf16[96,512,128]{2,1,0:T(8,128)(2,1)} fusion(bf16[512,32,128]{2,0,1:T(8,128)(2,1)} %copy.28, s32[1024]{0:T(1024)S(1)} %pad_clamp_fusion.5), kind=kCustom, calls=%fused_computation.4 | custom fusion | bytes 25166208 | tf_op jit(solution)/shard_map/gather | solution.py:20
  69.8 9.7 %fusion.2 = bf16[1,512,8,128]{1,3,2,0:T(8,128)(2,1)} fusion(bf16[512,8,12,128]{3,0,2,1:T(8,128)(2,1)} %bitcast.177, bf16[12,128,128]{2,1,0:T(8,128)(2,1)S(1)} %gather_fusion.2), kind=kOutput, calls=%fused_computation.26 | convolution fusion | flops 1611137024 | bytes 14024704 | tf_op jit(solution)/shard_map/pajkc,krc->pajr/dot_general | solution.py:22
  79.6 9.0 %gather_fusion.5 = bf16[96,512,128]{2,1,0:T(8,128)(2,1)} fusion(bf16[512,32,128]{2,0,1:T(8,128)(2,1)} %copy.28, s32[1024]{0:T(1024)S(1)} %pad_clamp_fusion.4), kind=kCustom, calls=%fused_computation.5 | custom fusion | bytes 25166208 | tf_op jit(solution)/shard_map/gather | solution.py:20
  88.6 8.8 %fusion.3 = bf16[1,512,8,128]{1,3,2,0:T(8,128)(2,1)S(1)} fusion(bf16[512,8,12,128]{3,0,2,1:T(8,128)(2,1)} %bitcast.176, bf16[12,128,128]{2,1,0:T(8,128)(2,1)S(1)} %gather_fusion.2), kind=kOutput, calls=%fused_computation.27 | convolution fusion | flops 1611137024 | bytes 14024704 | tf_op jit(solution)/shard_map/pajkc,krc->pajr/dot_general | solution.py:22
  97.5 0.6 pad_maximum_fusion
  98.0 36.5 %copy.56 = bf16[1,512,4096]{1,0,2:T(2,128)(2,1)} copy(bf16[1,512,4096]{1,2,0:T(8,128)(2,1)S(1)} %bitcast.178) | data formatting | bytes 8388608 | tf_op jit(solution)/shard_map/reshape | solution.py:26
  134.5 0.5 broadcast.272
  135.0 28.5 %reduce.4 = bf16[4096,512]{1,0:T(8,128)(2,1)} reduce(bf16[4096,1,512]{2,1,0:T(2,128)(2,1)} %bitcast.172, bf16[]{:T(256)} %broadcast.272), dimensions={1}, to_apply=%bitcast.167.reduce_sub_computation | reduce | bytes 8388610
  163.5 7.9 %reshape.535 = bf16[8,2,131072]{2,1,0:T(2,128)(2,1)} reshape(bf16[4096,512]{1,0:T(8,128)(2,1)} %reduce.4) | data formatting | bytes 8388608
  171.4 7.3 %all-to-all-start = ((bf16[8,2,131072]{2,1,0:T(2,128)(2,1)}), bf16[8,2,131072]{2,1,0:T(2,128)(2,1)}, u32[]{:S(2)}, u32[]{:S(2)}) async-start(bf16[8,2,131072]{2,1,0:T(2,128)(2,1)} %reshape.535), calls=%async_computation | async-start | bytes 8388608 | tf_op jit(solution)/shard_map/all_to_all | solution.py:74
  178.8 0.1 constant_dynamic-slice_fusion.2
  179.1 0.1 reshape.463
  179.4 0.1 reshape.483
  179.5 0.1 reshape.493
  179.6 0.6 gather_fusion
  180.3 91.7 %all-to-all-done = bf16[8,2,131072]{2,1,0:T(2,128)(2,1)} async-done(((bf16[8,2,131072]{2,1,0:T(2,128)(2,1)}), bf16[8,2,131072]{2,1,0:T(2,128)(2,1)}, u32[]{:S(2)}, u32[]{:S(2)}) %all-to-all-start) | async-done | bytes 4194336 | tf_op jit(solution)/shard_map/all_to_all | solution.py:74
  272.0 8.8 %reshape.536 = bf16[4096,1,512]{2,1,0:T(2,128)(2,1)} reshape(bf16[8,2,131072]{2,1,0:T(2,128)(2,1)} %all-to-all-done) | data formatting | bytes 8388608
  280.8 6.6 %copy.43 = bf16[1,512,4096]{1,2,0:T(8,128)(2,1)} copy(bf16[1,512,4096]{1,0,2:T(2,128)(2,1)} %bitcast.173) | data formatting | bytes 8388608
  287.4 6.5 %copy.33 = bf16[1,8,512,512]{3,2,1,0:T(8,128)(2,1)} copy(bf16[1,8,512,512]{2,3,1,0:T(8,128)(2,1)} %bitcast.179) | data formatting | bytes 8388608 | tf_op jit(solution)/shard_map/all_to_all | solution.py:74
  293.9 3.9 multiply_bitcast_fusion
  297.8 9.0 %gather_fusion.6 = bf16[96,128,512]{2,1,0:T(8,128)(2,1)} fusion(bf16[32,128,512]{2,1,0:T(8,128)(2,1)} %multiply_bitcast_fusion, s32[1024]{0:T(1024)S(1)} %pad_clamp_fusion.3), kind=kCustom, calls=%fused_computation.6 | custom fusion | bytes 25166208 | tf_op jit(solution)/shard_map/gather | solution.py:42
  306.8 9.0 %gather_fusion.7 = bf16[96,128,512]{2,1,0:T(8,128)(2,1)} fusion(bf16[32,128,512]{2,1,0:T(8,128)(2,1)} %multiply_bitcast_fusion, s32[1024]{0:T(1024)S(1)} %pad_clamp_fusion.2), kind=kCustom, calls=%fused_computation.7 | custom fusion | bytes 25166208 | tf_op jit(solution)/shard_map/gather | solution.py:42
  315.8 5.9 %fusion.4 = bf16[1,8,128,512]{3,2,1,0:T(8,128)(2,1)S(1)} fusion(bf16[8,12,128,512]{3,2,1,0:T(8,128)(2,1)} %bitcast.168, bf16[12,128,128]{2,1,0:T(8,128)(2,1)S(1)} %gather_fusion), kind=kOutput, calls=%fused_computation.28 | convolution fusion | flops 1611137024 | bytes 14024704 | tf_op jit(solution)/shard_map/pjkcn,krc->pjrn/dot_general | solution.py:44
  321.7 2.3 copy-done.2
  324.0 3.0 fusion.5
  327.0 9.0 %gather_fusion.8 = bf16[96,128,512]{2,1,0:T(8,128)(2,1)} fusion(bf16[32,128,512]{2,1,0:T(8,128)(2,1)} %multiply_bitcast_fusion, s32[1024]{0:T(1024)S(1)} %pad_clamp_fusion.1), kind=kCustom, calls=%fused_computation.8 | custom fusion | bytes 25166208 | tf_op jit(solution)/shard_map/gather | solution.py:42
  336.0 6.7 %fusion.6 = bf16[1,8,128,512]{3,2,1,0:T(8,128)(2,1)} fusion(bf16[8,12,128,512]{3,2,1,0:T(8,128)(2,1)} %bitcast.171, bf16[12,128,128]{2,1,0:T(8,128)(2,1)S(1)} %gather_fusion), kind=kOutput, calls=%fused_computation.30 | convolution fusion | flops 1611137024 | bytes 14024704 | tf_op jit(solution)/shard_map/pjkcn,krc->pjrn/dot_general | solution.py:44
  342.6 9.0 %gather_fusion.9 = bf16[96,128,512]{2,1,0:T(8,128)(2,1)} fusion(bf16[32,128,512]{2,1,0:T(8,128)(2,1)} %multiply_bitcast_fusion, s32[1024]{0:T(1024)S(1)} %pad_clamp_fusion), kind=kCustom, calls=%fused_computation.9 | custom fusion | bytes 25166208 | tf_op jit(solution)/shard_map/gather | solution.py:42
  351.7 5.9 %fusion.7 = bf16[1,8,128,512]{3,2,1,0:T(8,128)(2,1)S(1)} fusion(bf16[8,12,128,512]{3,2,1,0:T(8,128)(2,1)} %bitcast.170, bf16[12,128,128]{2,1,0:T(8,128)(2,1)S(1)} %gather_fusion), kind=kOutput, calls=%fused_computation.31 | convolution fusion | flops 1611137024 | bytes 14024704 | tf_op jit(solution)/shard_map/pjkcn,krc->pjrn/dot_general | solution.py:44
  357.6 0.6 pad_maximum_fusion.1
  358.2 5.1 %select_convert_fusion = bf16[2,4096,512]{2,1,0:T(8,128)(2,1)} fusion(bf16[4096,512]{1,0:T(8,128)(2,1)S(1)} %bitcast.182, pred[2]{0:T(512)(128)(4,1)S(1)} %iota_compare_fusion), kind=kLoop, calls=%fused_computation.10 | loop fusion | flops 4194304 | bytes 12582914 | tf_op jit(solution)/shard_map/convert_element_type | solution.py:84
  363.3 70.7 %reduce-scatter.2.cloned.1.call-done = bf16[2,1024,512]{2,1,0:T(8,128)(2,1)} async-done(((bf16[2,4096,512]{2,1,0:T(8,128)(2,1)}), bf16[2,1024,512]{2,1,0:T(8,128)(2,1)}) %reduce-scatter.2.cloned.1.call-update) | async-done | bytes 2097168 | tf_op jit(solution)/shard_map/reduce_scatter | solution.py:83
  433.9 4.2 convert_element_type.112
  (54 shorter events, 0.9 us)
Async XLA Ops:
  6.5 40.3 %copy-start = (bf16[16,128,128]{2,1,0:T(8,128)(2,1)S(1)}, bf16[16,128,128]{2,1,0:T(8,128)(2,1)}, u32[]{:S(2)}) copy-start(bf16[16,128,128]{2,1,0:T(8,128)(2,1)} %param.16) | copy-start | bytes 1572868
  6.5 11.2 %copy-start.10 = (s32[2,4096]{1,0:T(2,128)S(1)}, s32[2,4096]{1,0:T(2,128)}, u32[]{:S(2)}) copy-start(s32[2,4096]{1,0:T(2,128)} %param.15) | copy-start | bytes 98308
  6.5 11.2 %copy-start.11 = (s32[2,4096]{1,0:T(2,128)S(1)}, s32[2,4096]{1,0:T(2,128)}, u32[]{:S(2)}) copy-start(s32[2,4096]{1,0:T(2,128)} %param.12) | copy-start | bytes 98308
  17.9 10.4 %copy-start.8 = (s32[2,32,12]{1,0,2:T(2,128)S(1)}, s32[2,32,12]{1,0,2:T(2,128)}, u32[]{:S(2)}) copy-start(s32[2,32,12]{1,0,2:T(2,128)} %param.10) | copy-start | bytes 9220
  17.9 10.8 %copy-start.12 = (s32[2,12]{1,0:T(2,128)S(1)}, s32[2,12]{1,0:T(2,128)}, u32[]{:S(2)}) copy-start(s32[2,12]{1,0:T(2,128)} %param.14) | copy-start | bytes 292
  17.9 10.8 %copy-start.13 = (s32[2,12]{1,0:T(2,128)S(1)}, s32[2,12]{1,0:T(2,128)}, u32[]{:S(2)}) copy-start(s32[2,12]{1,0:T(2,128)} %param.11) | copy-start | bytes 292
  47.4 8.9 %copy-start.3 = (bf16[96,512,128]{2,1,0:T(8,128)(2,1)S(1)}, bf16[96,512,128]{2,1,0:T(8,128)(2,1)}, u32[]{:S(2)}) copy-start(bf16[96,512,128]{2,1,0:T(8,128)(2,1)} %gather_fusion.3) | copy-start | bytes 37748740
  88.6 8.8 %copy-start.6 = (bf16[1,512,8,128]{1,3,2,0:T(8,128)(2,1)S(1)}, bf16[1,512,8,128]{1,3,2,0:T(8,128)(2,1)}, u32[]{:S(2)}) copy-start(bf16[1,512,8,128]{1,3,2,0:T(8,128)(2,1)} %fusion.2) | copy-start | bytes 3145732
  163.5 15.2 %copy-start.9 = (s32[2,32,12]{1,0,2:T(2,128)S(1)}, s32[2,32,12]{1,0,2:T(2,128)}, u32[]{:S(2)}) copy-start(s32[2,32,12]{1,0,2:T(2,128)} %param.13) | copy-start | bytes 9220
  163.5 16.0 %copy-start.7 = (bf16[16,128,128]{2,1,0:T(8,128)(2,1)S(1)}, bf16[16,128,128]{2,1,0:T(8,128)(2,1)}, u32[]{:S(2)}) copy-start(bf16[16,128,128]{2,1,0:T(8,128)(2,1)} %param.17) | copy-start | bytes 1572868
  171.4 100.6 %all-to-all-start = ((bf16[8,2,131072]{2,1,0:T(2,128)(2,1)}), bf16[8,2,131072]{2,1,0:T(2,128)(2,1)}, u32[]{:S(2)}, u32[]{:S(2)}) async-start(bf16[8,2,131072]{2,1,0:T(2,128)(2,1)} %reshape.535), calls=%async_computation | async-start | bytes 8388608 | tf_op jit(solution)/shard_map/all_to_all | solution.py:74
  178.7 255.2 %reduce-scatter.2.cloned.1.call-start = ((), (), s32[]{:S(2)}) async-start(), calls=%async_computation.2 | async-start | bytes 10485760 | tf_op jit(solution)/shard_map/reduce_scatter | solution.py:83
  315.8 8.2 %copy-start.2 = (bf16[96,128,512]{2,1,0:T(8,128)(2,1)S(1)}, bf16[96,128,512]{2,1,0:T(8,128)(2,1)}, u32[]{:S(2)}) copy-start(bf16[96,128,512]{2,1,0:T(8,128)(2,1)} %gather_fusion.7) | copy-start | bytes 37748740
  351.7 5.9 %copy-start.4 = (bf16[1,8,128,512]{3,2,1,0:T(8,128)(2,1)S(1)}, bf16[1,8,128,512]{3,2,1,0:T(8,128)(2,1)}, u32[]{:S(2)}) copy-start(bf16[1,8,128,512]{3,2,1,0:T(8,128)(2,1)} %fusion.5) | copy-start | bytes 3145732
  351.7 5.9 %copy-start.5 = (bf16[1,8,128,512]{3,2,1,0:T(8,128)(2,1)S(1)}, bf16[1,8,128,512]{3,2,1,0:T(8,128)(2,1)}, u32[]{:S(2)}) copy-start(bf16[1,8,128,512]{3,2,1,0:T(8,128)(2,1)} %fusion.6) | copy-start | bytes 3145732
  358.1 80.0 %copy-start.1 = (bf16[16,128,128]{2,1,0:T(8,128)(2,1)S(1)}, bf16[16,128,128]{2,1,0:T(8,128)(2,1)}, u32[]{:S(2)}) copy-start(bf16[16,128,128]{2,1,0:T(8,128)(2,1)} %param.16) | copy-start | bytes 1572868
Sparse Core Ops, SparseCore 0:
  363.4 70.5 reduce-scatter.1
where the time goes:
time: 446 us; the launch traced here: 445 us
  local copies, waits for them, and re-layouts  162 us (36%)
  waiting for transfers between devices  162 us (36%)
  matrix products  52.9 us (12%)
  other arithmetic  47.1 us (11%)
  between operations  13.7 us (3%)
  starting transfers between devices  7.33 us (2%)
    all_to_all x1, waiting for transfers between devices, local(): lax.all_to_all(half, 'str', split_axis=2, concat_axis=1, tiled=True)  91.7 us
    reduce_scatter x1, waiting for transfers between devices, local(): lax.psum_scatter(padded.astype(jnp.bfloat16), 'fac', scatter_dimension=1,...  70.7 us
    reshape x1, local copies, waits for them, and re-layouts, apply_beta(): jnp.concatenate(pieces, axis=2).reshape(part_count, height, column_count)  36.5 us
    gather x4, local copies, waits for them, and re-layouts, apply_beta(): gathered = blocks[:, :, chosen]  36.1 us
    gather x4, local copies, waits for them, and re-layouts, apply_alpha(): gathered = blocks[:, chosen]  36 us
    unnamed x41, local copies, waits for them, and re-layouts  33.3 us
    dot_general x4, matrix products, apply_beta(): jnp.einsum('pajkc,krc->pajr', gathered, weights, preferred_element_type=j...  31.5 us
    unnamed x1, other arithmetic  28.5 us
  transfers between devices with their start and end apart: 2, of which 2 were waited for; matrix products, arithmetic and copies ran while one was open for 0% of the time, Pallas kernels for 0%

commit v1 on v0

--- a/solution.py
+++ b/solution.py
@@ -2,6 +2,13 @@
 import jax.numpy as jnp
 from jax import lax
 from jax.sharding import PartitionSpec as P
+
+
+def stacked_exchange(x, mesh_axis, split, join):
+    peers = lax.axis_size(mesh_axis)
+    blocks = jnp.stack(jnp.split(x, peers, axis=split), axis=0)
+    blocks = lax.all_to_all(blocks, mesh_axis, split_axis=0, concat_axis=0)
+    return jnp.concatenate(blocks, axis=join)
 
 
 def apply_beta(amplitudes, block_ids, tile_ids, flips, tile_table):
@@ -71,11 +78,7 @@
     alpha_kinds = lax.dynamic_index_in_dim(alpha_tile, factor, 0, keepdims=False)
     alpha_signs = lax.dynamic_index_in_dim(alpha_flip, factor, 0, keepdims=False)
     mixed = apply_alpha(
-        lax.all_to_all(half, "str", split_axis=2, concat_axis=1, tiled=True),
-        alpha_ids,
-        alpha_kinds,
-        alpha_signs,
-        alpha_tiles,
+        stacked_exchange(half, "str", 2, 1), alpha_ids, alpha_kinds, alpha_signs, alpha_tiles
     )
     mixed = lax.optimization_barrier(mixed)
     selector = (jnp.arange(2) == part)[:, None, None]

time: 446 us -> 368 us (0.83)
  local copies, waits for them, and re-layouts: 162 us -> 112 us
  other arithmetic: 47.1 us -> 18.6 us
    reshape x1 -> x0, local copies, waits for them, and re-layouts: 36.5 us -> none  [apply_beta(): jnp.concatenate(pieces, axis=2).reshape(part_count, height, column_count)]
    unnamed x1 -> x0, other arithmetic: 28.5 us -> none
    unnamed x41 -> x52, local copies, waits for them, and re-layouts: 33.3 us -> 24.6 us
    all_to_all x1 -> x0, local copies, waits for them, and re-layouts: 6.46 us -> none  [local(): lax.all_to_all(half, 'str', split_axis=2, concat_axis=1, tiled=True)]
where the time goes in v1:
time: 368 us; the launch traced here: 367 us
  waiting for transfers between devices  162 us (44%)
  local copies, waits for them, and re-layouts  112 us (30%)
  matrix products  52.9 us (14%)
  other arithmetic  18.6 us (5%)
  between operations  13.7 us (4%)
  starting transfers between devices  7.45 us (2%)
    all_to_all x1, waiting for transfers between devices, stacked_exchange(): blocks = lax.all_to_all(blocks, mesh_axis, split_axis=0, concat_axis=0)  91.7 us
    reduce_scatter x1, waiting for transfers between devices, local(): lax.psum_scatter(padded.astype(jnp.bfloat16), 'fac', scatter_dimension=1,...  70.7 us
    gather x4, local copies, waits for them, and re-layouts, apply_beta(): gathered = blocks[:, :, chosen]  36.1 us
    gather x4, local copies, waits for them, and re-layouts, apply_alpha(): gathered = blocks[:, chosen]  36.1 us
    dot_general x4, matrix products, apply_beta(): jnp.einsum('pajkc,krc->pajr', gathered, weights, preferred_element_type=j...  31.6 us
    unnamed x52, local copies, waits for them, and re-layouts  24.6 us
    dot_general x4, matrix products, apply_alpha(): jnp.einsum('pjkcn,krc->pjrn', gathered, weights, preferred_element_type=j...  21.4 us
    all_to_all x1, starting transfers between devices, stacked_exchange(): blocks = lax.all_to_all(blocks, mesh_axis, split_axis=0, concat_axis=0)  7.41 us
  transfers between devices with their start and end apart: 2, of which 2 were waited for; matrix products, arithmetic and copies ran while one was open for 0% of the time, Pallas kernels for 0%

profile of v1, /device:TPU:0, one launch (start us, length us, event | category | flops | bytes accessed | tf_op | source)
XLA Modules:
  0.0 367.3 jit_solution(14059652385584747454)
XLA Ops:
  6.5 4.8 %constant_dynamic-slice_fusion.9 = bf16[1,512,4096]{2,1,0:T(8,128)(2,1)} fusion(bf16[2,512,4096]{2,1,0:T(8,128)(2,1)} %param.9, s32[]{:T(128)S(6)} %select_n.134), kind=kLoop, calls=%fused_computation.77 | loop fusion | bytes 8388612 | tf_op jit(solution)/shard_map/jit(dynamic_index_in_dim)/dynamic_slice | solution.py:72
  11.3 6.5 %copy.64 = bf16[1,512,4096]{1,2,0:T(8,128)(2,1)} copy(bf16[1,512,4096]{2,1,0:T(8,128)(2,1)} %constant_dynamic-slice_fusion.9) | data formatting | bytes 8388608
  17.8 3.9 %broadcast_multiply_fusion = bf16[1,512,4096]{1,2,0:T(8,128)(2,1)} fusion(bf16[1,512,4096]{1,2,0:T(8,128)(2,1)} %copy.64, bf16[4096]{0:T(1024)(128)(2,1)S(1)} %convert_reduce_fusion.1), kind=kLoop, calls=%fused_computation.23 | loop fusion | flops 2097152 | bytes 8396800 | tf_op jit(solution)/shard_map/mul | solution.py:19
  21.8 6.5 %copy.43 = bf16[512,32,128]{2,0,1:T(8,128)(2,1)} copy(bf16[512,32,128]{0,2,1:T(8,128)(2,1)} %bitcast.185) | data formatting | bytes 8388608 | tf_op jit(solution)/shard_map/reshape | solution.py:20
  28.8 9.0 %gather_fusion.1 = bf16[96,512,128]{2,1,0:T(8,128)(2,1)} fusion(bf16[512,32,128]{2,0,1:T(8,128)(2,1)} %copy.43, s32[1024]{0:T(1024)S(1)} %pad_clamp_fusion.8), kind=kCustom, calls=%fused_computation.1 | custom fusion | bytes 25166208 | tf_op jit(solution)/shard_map/gather | solution.py:27
  37.8 9.0 %gather_fusion.3 = bf16[96,512,128]{2,1,0:T(8,128)(2,1)} fusion(bf16[512,32,128]{2,0,1:T(8,128)(2,1)} %copy.43, s32[1024]{0:T(1024)S(1)} %pad_clamp_fusion.6), kind=kCustom, calls=%fused_computation.3 | custom fusion | bytes 25166208 | tf_op jit(solution)/shard_map/gather | solution.py:27
  46.8 0.6 gather_fusion.2
  47.4 8.9 %fusion = bf16[1,512,8,128]{1,3,2,0:T(8,128)(2,1)S(1)} fusion(bf16[512,8,12,128]{3,0,2,1:T(8,128)(2,1)} %bitcast.181, bf16[12,128,128]{2,1,0:T(8,128)(2,1)S(1)} %gather_fusion.2), kind=kOutput, calls=%fused_computation.24 | convolution fusion | flops 1611137024 | bytes 14024704 | tf_op jit(solution)/shard_map/pajkc,krc->pajr/dot_general | solution.py:29
  56.3 4.2 %fusion.1 = bf16[1,512,8,128]{1,3,2,0:T(8,128)(2,1)S(1)} fusion(bf16[512,8,12,128]{3,0,2,1:T(8,128)(2,1)S(1)} %bitcast.182, bf16[12,128,128]{2,1,0:T(8,128)(2,1)S(1)} %gather_fusion.2), kind=kOutput, calls=%fused_computation.25 | convolution fusion | flops 1611137024 | bytes 14024704 | tf_op jit(solution)/shard_map/pajkc,krc->pajr/dot_general | solution.py:29
  60.8 9.0 %gather_fusion.4 = bf16[96,512,128]{2,1,0:T(8,128)(2,1)} fusion(bf16[512,32,128]{2,0,1:T(8,128)(2,1)} %copy.43, s32[1024]{0:T(1024)S(1)} %pad_clamp_fusion.5), kind=kCustom, calls=%fused_computation.4 | custom fusion | bytes 25166208 | tf_op jit(solution)/shard_map/gather | solution.py:27
  69.8 9.7 %fusion.2 = bf16[1,512,8,128]{1,3,2,0:T(8,128)(2,1)} fusion(bf16[512,8,12,128]{3,0,2,1:T(8,128)(2,1)} %bitcast.184, bf16[12,128,128]{2,1,0:T(8,128)(2,1)S(1)} %gather_fusion.2), kind=kOutput, calls=%fused_computation.26 | convolution fusion | flops 1611137024 | bytes 14024704 | tf_op jit(solution)/shard_map/pajkc,krc->pajr/dot_general | solution.py:29
  79.6 9.0 %gather_fusion.5 = bf16[96,512,128]{2,1,0:T(8,128)(2,1)} fusion(bf16[512,32,128]{2,0,1:T(8,128)(2,1)} %copy.43, s32[1024]{0:T(1024)S(1)} %pad_clamp_fusion.4), kind=kCustom, calls=%fused_computation.5 | custom fusion | bytes 25166208 | tf_op jit(solution)/shard_map/gather | solution.py:27
  88.6 8.8 %fusion.3 = bf16[1,512,8,128]{1,3,2,0:T(8,128)(2,1)S(1)} fusion(bf16[512,8,12,128]{3,0,2,1:T(8,128)(2,1)} %bitcast.183, bf16[12,128,128]{2,1,0:T(8,128)(2,1)S(1)} %gather_fusion.2), kind=kOutput, calls=%fused_computation.27 | convolution fusion | flops 1611137024 | bytes 14024704 | tf_op jit(solution)/shard_map/pajkc,krc->pajr/dot_general | solution.py:29
  97.5 0.6 pad_maximum_fusion
  98.0 1.4 fusion.20
  99.5 2.1 copy.70
  101.5 1.9 bitcast_dynamic-update-slice_fusion.7
  103.4 2.1 copy.71
  105.5 1.0 copy.72
  106.5 0.2 copy.73
  106.7 0.2 copy.74
  106.9 0.2 copy.75
  107.1 0.2 copy.76
  107.3 0.2 copy.77
  107.6 1.9 bitcast_dynamic-update-slice_fusion.6
  109.4 1.9 bitcast_dynamic-update-slice_fusion.5
  111.3 0.8 bitcast_dynamic-update-slice_fusion.4
  112.1 0.8 bitcast_dynamic-update-slice_fusion.3
  113.0 0.8 bitcast_dynamic-update-slice_fusion.2
  113.8 0.8 bitcast_dynamic-update-slice_fusion.1
  114.6 0.8 bitcast_dynamic-update-slice_fusion
  115.4 7.4 %all-to-all-start = ((bf16[8,1,512,512]{3,2,1,0:T(8,128)(2,1)}), bf16[8,1,512,512]{3,2,1,0:T(8,128)(2,1)}, u32[]{:S(2)}, u32[]{:S(2)}) async-start(bf16[8,1,512,512]{3,2,1,0:T(8,128)(2,1)} %bitcast_dynamic-update-slice_fusion), calls=%async_computation | async-start | bytes 8388608 | tf_op jit(solution)/shard_map/all_to_all | solution.py:10
  123.7 0.6 gather_fusion
  124.5 91.7 %all-to-all-done = bf16[8,1,512,512]{3,2,1,0:T(8,128)(2,1)} async-done(((bf16[8,1,512,512]{3,2,1,0:T(8,128)(2,1)}), bf16[8,1,512,512]{3,2,1,0:T(8,128)(2,1)}, u32[]{:S(2)}, u32[]{:S(2)}) %all-to-all-start) | async-done | bytes 4194336 | tf_op jit(solution)/shard_map/all_to_all | solution.py:10
  216.1 3.9 %multiply_bitcast_fusion = bf16[32,128,512]{2,1,0:T(8,128)(2,1)} fusion(bf16[1,32,128,512]{3,2,1,0:T(8,128)(2,1)} %bitcast.40, bf16[32,128]{1,0:T(8,128)(2,1)S(1)} %bitcast.188), kind=kLoop, calls=%fused_computation.14 | loop fusion | flops 2097152 | bytes 8396800 | tf_op jit(solution)/shard_map/mul | solution.py:41
  220.1 9.0 %gather_fusion.6 = bf16[96,128,512]{2,1,0:T(8,128)(2,1)} fusion(bf16[32,128,512]{2,1,0:T(8,128)(2,1)} %multiply_bitcast_fusion, s32[1024]{0:T(1024)S(1)} %pad_clamp_fusion.3), kind=kCustom, calls=%fused_computation.6 | custom fusion | bytes 25166208 | tf_op jit(solution)/shard_map/gather | solution.py:49
  229.1 9.0 %gather_fusion.7 = bf16[96,128,512]{2,1,0:T(8,128)(2,1)} fusion(bf16[32,128,512]{2,1,0:T(8,128)(2,1)} %multiply_bitcast_fusion, s32[1024]{0:T(1024)S(1)} %pad_clamp_fusion.2), kind=kCustom, calls=%fused_computation.7 | custom fusion | bytes 25166208 | tf_op jit(solution)/shard_map/gather | solution.py:49
  238.1 5.9 %fusion.4 = bf16[1,8,128,512]{3,2,1,0:T(8,128)(2,1)S(1)} fusion(bf16[8,12,128,512]{3,2,1,0:T(8,128)(2,1)} %bitcast.177, bf16[12,128,128]{2,1,0:T(8,128)(2,1)S(1)} %gather_fusion), kind=kOutput, calls=%fused_computation.28 | convolution fusion | flops 1611137024 | bytes 14024704 | tf_op jit(solution)/shard_map/pjkcn,krc->pjrn/dot_general | solution.py:51
  244.0 2.3 copy-done.2
  246.3 3.0 fusion.5
  249.3 9.0 %gather_fusion.8 = bf16[96,128,512]{2,1,0:T(8,128)(2,1)} fusion(bf16[32,128,512]{2,1,0:T(8,128)(2,1)} %multiply_bitcast_fusion, s32[1024]{0:T(1024)S(1)} %pad_clamp_fusion.1), kind=kCustom, calls=%fused_computation.8 | custom fusion | bytes 25166208 | tf_op jit(solution)/shard_map/gather | solution.py:49
  258.3 6.7 %fusion.6 = bf16[1,8,128,512]{3,2,1,0:T(8,128)(2,1)} fusion(bf16[8,12,128,512]{3,2,1,0:T(8,128)(2,1)} %bitcast.180, bf16[12,128,128]{2,1,0:T(8,128)(2,1)S(1)} %gather_fusion), kind=kOutput, calls=%fused_computation.30 | convolution fusion | flops 1611137024 | bytes 14024704 | tf_op jit(solution)/shard_map/pjkcn,krc->pjrn/dot_general | solution.py:51
  264.9 9.0 %gather_fusion.9 = bf16[96,128,512]{2,1,0:T(8,128)(2,1)} fusion(bf16[32,128,512]{2,1,0:T(8,128)(2,1)} %multiply_bitcast_fusion, s32[1024]{0:T(1024)S(1)} %pad_clamp_fusion), kind=kCustom, calls=%fused_computation.9 | custom fusion | bytes 25166208 | tf_op jit(solution)/shard_map/gather | solution.py:49
  274.0 5.9 %fusion.7 = bf16[1,8,128,512]{3,2,1,0:T(8,128)(2,1)S(1)} fusion(bf16[8,12,128,512]{3,2,1,0:T(8,128)(2,1)} %bitcast.179, bf16[12,128,128]{2,1,0:T(8,128)(2,1)S(1)} %gather_fusion), kind=kOutput, calls=%fused_computation.31 | convolution fusion | flops 1611137024 | bytes 14024704 | tf_op jit(solution)/shard_map/pjkcn,krc->pjrn/dot_general | solution.py:51
  279.9 0.6 pad_maximum_fusion.1
  280.4 5.1 %select_convert_fusion = bf16[2,4096,512]{2,1,0:T(8,128)(2,1)} fusion(bf16[4096,512]{1,0:T(8,128)(2,1)S(1)} %bitcast.187, pred[2]{0:T(512)(128)(4,1)S(1)} %iota_compare_fusion), kind=kLoop, calls=%fused_computation.10 | loop fusion | flops 4194304 | bytes 12582914 | tf_op jit(solution)/shard_map/convert_element_type | solution.py:87
  285.6 70.7 %reduce-scatter.2.cloned.1.call-done = bf16[2,1024,512]{2,1,0:T(8,128)(2,1)} async-done(((bf16[2,4096,512]{2,1,0:T(8,128)(2,1)}), bf16[2,1024,512]{2,1,0:T(8,128)(2,1)}) %reduce-scatter.2.cloned.1.call-update) | async-done | bytes 2097168 | tf_op jit(solution)/shard_map/reduce_scatter | solution.py:86
  356.3 4.2 %convert_element_type.112 = f32[2,1024,512]{2,1,0:T(8,128)} convert(bf16[2,1024,512]{2,1,0:T(8,128)(2,1)} %reduce-scatter.2.cloned.1.call-done) | non-fusion elementwise | flops 1048576 | bytes 6291456 | tf_op jit(solution)/shard_map/convert_element_type | solution.py:88
  (65 shorter events, 1.9 us)
Async XLA Ops:
  6.5 40.3 %copy-start = (bf16[16,128,128]{2,1,0:T(8,128)(2,1)S(1)}, bf16[16,128,128]{2,1,0:T(8,128)(2,1)}, u32[]{:S(2)}) copy-start(bf16[16,128,128]{2,1,0:T(8,128)(2,1)} %param.16) | copy-start | bytes 1572868
  11.3 6.5 %copy-start.10 = (s32[2,4096]{1,0:T(2,128)S(1)}, s32[2,4096]{1,0:T(2,128)}, u32[]{:S(2)}) copy-start(s32[2,4096]{1,0:T(2,128)} %param.12) | copy-start | bytes 98308
  21.8 6.5 %copy-start.8 = (s32[2,32,12]{1,0,2:T(2,128)S(1)}, s32[2,32,12]{1,0,2:T(2,128)}, u32[]{:S(2)}) copy-start(s32[2,32,12]{1,0,2:T(2,128)} %param.10) | copy-start | bytes 9220
  21.8 6.9 %copy-start.12 = (s32[2,12]{1,0:T(2,128)S(1)}, s32[2,12]{1,0:T(2,128)}, u32[]{:S(2)}) copy-start(s32[2,12]{1,0:T(2,128)} %param.14) | copy-start | bytes 292
  21.8 6.9 %copy-start.13 = (s32[2,12]{1,0:T(2,128)S(1)}, s32[2,12]{1,0:T(2,128)}, u32[]{:S(2)}) copy-start(s32[2,12]{1,0:T(2,128)} %param.11) | copy-start | bytes 292
  47.4 8.9 %copy-start.3 = (bf16[96,512,128]{2,1,0:T(8,128)(2,1)S(1)}, bf16[96,512,128]{2,1,0:T(8,128)(2,1)}, u32[]{:S(2)}) copy-start(bf16[96,512,128]{2,1,0:T(8,128)(2,1)} %gather_fusion.3) | copy-start | bytes 37748740
  88.6 8.8 %copy-start.6 = (bf16[1,512,8,128]{1,3,2,0:T(8,128)(2,1)S(1)}, bf16[1,512,8,128]{1,3,2,0:T(8,128)(2,1)}, u32[]{:S(2)}) copy-start(bf16[1,512,8,128]{1,3,2,0:T(8,128)(2,1)} %fusion.2) | copy-start | bytes 3145732
  115.4 7.5 %copy-start.9 = (s32[2,32,12]{1,0,2:T(2,128)S(1)}, s32[2,32,12]{1,0,2:T(2,128)}, u32[]{:S(2)}) copy-start(s32[2,32,12]{1,0,2:T(2,128)} %param.13) | copy-start | bytes 9220
  115.4 8.3 %copy-start.7 = (bf16[16,128,128]{2,1,0:T(8,128)(2,1)S(1)}, bf16[16,128,128]{2,1,0:T(8,128)(2,1)}, u32[]{:S(2)}) copy-start(bf16[16,128,128]{2,1,0:T(8,128)(2,1)} %param.17) | copy-start | bytes 1572868
  115.4 8.9 %copy-start.11 = (s32[2,4096]{1,0:T(2,128)S(1)}, s32[2,4096]{1,0:T(2,128)}, u32[]{:S(2)}) copy-start(s32[2,4096]{1,0:T(2,128)} %param.15) | copy-start | bytes 98308
  115.4 100.7 %all-to-all-start = ((bf16[8,1,512,512]{3,2,1,0:T(8,128)(2,1)}), bf16[8,1,512,512]{3,2,1,0:T(8,128)(2,1)}, u32[]{:S(2)}, u32[]{:S(2)}) async-start(bf16[8,1,512,512]{3,2,1,0:T(8,128)(2,1)} %bitcast_dynamic-update-slice_fusion), calls=%async_computation | async-start | bytes 8388608 | tf_op jit(solution)/shard_map/all_to_all | solution.py:10
  122.9 233.4 %reduce-scatter.2.cloned.1.call-start = ((), (), s32[]{:S(2)}) async-start(), calls=%async_computation.2 | async-start | bytes 10485760 | tf_op jit(solution)/shard_map/reduce_scatter | solution.py:86
  238.1 8.2 %copy-start.2 = (bf16[96,128,512]{2,1,0:T(8,128)(2,1)S(1)}, bf16[96,128,512]{2,1,0:T(8,128)(2,1)}, u32[]{:S(2)}) copy-start(bf16[96,128,512]{2,1,0:T(8,128)(2,1)} %gather_fusion.7) | copy-start | bytes 37748740
  274.0 5.9 %copy-start.4 = (bf16[1,8,128,512]{3,2,1,0:T(8,128)(2,1)S(1)}, bf16[1,8,128,512]{3,2,1,0:T(8,128)(2,1)}, u32[]{:S(2)}) copy-start(bf16[1,8,128,512]{3,2,1,0:T(8,128)(2,1)} %fusion.5) | copy-start | bytes 3145732
  274.0 5.9 %copy-start.5 = (bf16[1,8,128,512]{3,2,1,0:T(8,128)(2,1)S(1)}, bf16[1,8,128,512]{3,2,1,0:T(8,128)(2,1)}, u32[]{:S(2)}) copy-start(bf16[1,8,128,512]{3,2,1,0:T(8,128)(2,1)} %fusion.6) | copy-start | bytes 3145732
  285.6 74.9 %copy-start.1 = (bf16[16,128,128]{2,1,0:T(8,128)(2,1)S(1)}, bf16[16,128,128]{2,1,0:T(8,128)(2,1)}, u32[]{:S(2)}) copy-start(bf16[16,128,128]{2,1,0:T(8,128)(2,1)} %param.16) | copy-start | bytes 1572868
Sparse Core Ops, SparseCore 0:
  285.7 70.5 reduce-scatter.1
